TPU v7x, 32 devices: a whole 2x2x4 slice. The times are simulated.
32 devices in a mesh: ia: 4 (over z), ja: 4 (over x, core), ka: 2 (over y).
Axes of the slice: x: 2, y: 2, z: 4, core: 2. Of those that a mesh axis runs over, the one named last changes fastest.
Arguments:
- tensor: bfloat16 [64, 256, 512], P('ka', 'ia', 'ja'), may hold values from -768 to 768
- observed: int32 [64, 256, 512], P('ka', 'ia', 'ja'), may hold values from 0 to 1, as said below
- factor_a: bfloat16 [256, 128], P('ia', ('ja', 'ka')), may hold values from -6 to 6
- factor_b: bfloat16 [512, 128], P('ja', ('ia', 'ka')), may hold values from -6 to 6
- factor_c: bfloat16 [64, 128], P('ka', ('ia', 'ja')), may hold values from -6 to 6
Outputs:
- step_a: float32 [256, 128], P('ia', ('ja', 'ka'))
- step_b: float32 [512, 128], P('ja', ('ia', 'ka'))
- step_c: float32 [64, 128], P('ka', ('ia', 'ja'))
Inputs may be any that keep to these rules, and one draw needn't show every extreme that they name: `observed`: a 0/1 weight per cell.
All inputs are finite; a program needn't handle non-finite values.
Results may differ from a plain program's by a relative error of at most 0.0095.
Values may be sent and summed in bfloat16 or wider, within the bound.
A program may use at most 64 MiB of HBM per device.

v0:
```python
import jax
import jax.numpy as jnp
from jax import lax
from jax.sharding import PartitionSpec as P

ITERS = 2
DAMP = 1.0


def against(left_side, right_side):
    return lax.dot_general(
        left_side, right_side, (((1,), (1,)), ((), ())), preferred_element_type=jnp.float32
    )


def local(tensor, observed, factor_a, factor_b, factor_c):
    depth_rows, height_rows, width_cols = tensor.shape
    divisor = width_cols * lax.axis_size("ja") * (depth_rows * lax.axis_size("ka")) / 32.0
    full_a = lax.all_gather(factor_a, ("ja", "ka"), axis=1, tiled=True)
    full_b = lax.all_gather(factor_b, ("ia", "ka"), axis=1, tiled=True)
    full_c = lax.all_gather(factor_c, ("ia", "ja"), axis=1, tiled=True)
    columns = full_a.shape[1]
    wide_a = full_a.astype(jnp.float32)
    wide_c = full_c.astype(jnp.float32)
    weight = (observed.astype(jnp.float32) * (1.0 / divisor)).astype(jnp.bfloat16)
    weight = weight.reshape(depth_rows * height_rows, width_cols)
    paired = (
        (wide_c[:, None, :] * wide_a[None, :, :])
        .astype(jnp.bfloat16)
        .reshape(depth_rows * height_rows, columns)
    )

    def partials(weighted):
        part_b = lax.dot_general(
            weighted, paired, (((0,), (0,)), ((), ())), preferred_element_type=jnp.float32
        )
        mixture = jnp.dot(weighted, full_b, preferred_element_type=jnp.float32).reshape(
            depth_rows, height_rows, columns
        )
        part_a = jnp.einsum("kir,kr->ir", mixture, wide_c)
        part_c = jnp.einsum("kir,ir->kr", mixture, wide_a)
        return (part_a, part_b, part_c)

    def settle(parts):
        total_a = lax.psum(parts[0], ("ja", "ka"))
        total_b = lax.psum(parts[1], ("ia", "ka"))
        total_c = lax.psum(parts[2], ("ia", "ja"))
        return (total_a, total_b, total_c)

    scales = (
        1.0 / lax.axis_size(("ja", "ka")),
        1.0 / lax.axis_size(("ia", "ka")),
        1.0 / lax.axis_size(("ia", "ja")),
    )

    def inner_sum(first, second):
        local_sum = sum(
            (
                jnp.sum(left_side * right_side) * factor
                for left_side, right_side, factor in zip(first, second, scales)
            )
        )
        return lax.psum(local_sum, ("ia", "ja", "ka"))

    def expand(direction):
        hat_a = direction[0].astype(jnp.bfloat16)
        hat_b = direction[1].astype(jnp.bfloat16)
        hat_c = direction[2].astype(jnp.bfloat16)
        return (hat_a, hat_b, hat_c)

    def hessian_times(direction):
        hat_a, hat_b, hat_c = expand(direction)
        sideways = (
            hat_c.astype(jnp.float32)[:, None, :] * wide_a[None, :, :]
            + wide_c[:, None, :] * hat_a.astype(jnp.float32)[None, :, :]
        )
        sideways = sideways.astype(jnp.bfloat16).reshape(depth_rows * height_rows, columns)
        tangent = against(paired, hat_b) + against(sideways, full_b)
        weighted = (weight.astype(jnp.float32) * tangent).astype(jnp.bfloat16)
        parts = settle(partials(weighted))
        return tuple((part + DAMP * vector for part, vector in zip(parts, direction)))

    fitted = against(paired, full_b)
    values = tensor.reshape(depth_rows * height_rows, width_cols).astype(jnp.float32)
    errors = (weight.astype(jnp.float32) * (values - fitted)).astype(jnp.bfloat16)
    gradient = settle(partials(errors))
    solution = tuple((jnp.zeros_like(vector) for vector in gradient))
    residual = gradient
    direction = gradient
    norm_now = inner_sum(residual, residual)
    for iteration in range(ITERS):
        product = hessian_times(direction)
        step_size = norm_now / inner_sum(direction, product)
        solution = tuple(
            (vector + step_size * update for vector, update in zip(solution, direction))
        )
        if iteration + 1 < ITERS:
            residual = tuple(
                (vector - step_size * update for vector, update in zip(residual, product))
            )
            norm_next = inner_sum(residual, residual)
            direction = tuple(
                (
                    vector + norm_next / norm_now * update
                    for vector, update in zip(residual, direction)
                )
            )
            norm_now = norm_next
    position_a = lax.axis_index(("ja", "ka")) * factor_a.shape[1]
    position_b = lax.axis_index(("ia", "ka")) * factor_b.shape[1]
    position_c = lax.axis_index(("ia", "ja")) * factor_c.shape[1]
    step_a = lax.dynamic_slice_in_dim(solution[0], position_a, factor_a.shape[1], 1)
    step_b = lax.dynamic_slice_in_dim(solution[1], position_b, factor_b.shape[1], 1)
    step_c = lax.dynamic_slice_in_dim(solution[2], position_c, factor_c.shape[1], 1)
    return (step_a, step_b, step_c)


def solution(mesh):
    placed = (
        P("ka", "ia", "ja"),
        P("ka", "ia", "ja"),
        P("ia", ("ja", "ka")),
        P("ja", ("ia", "ka")),
        P("ka", ("ia", "ja")),
    )
    return jax.shard_map(
        local,
        mesh=mesh,
        in_specs=placed,
        out_specs=(P("ia", ("ja", "ka")), P("ja", ("ia", "ka")), P("ka", ("ia", "ja"))),
        check_vma=False,
    )
```

profile of v0, /device:TPU:0, one launch (start us, length us, event | category | flops | bytes accessed | tf_op | source)
XLA Modules:
  0.0 519.4 jit_solution(12304898515846047202)
XLA Ops:
  7.2 14.5 %all_gather.10 = bf16[64,128]{0,1:T(8,128)(2,1)S(1)} all-gather(bf16[64,16]{0,1:T(8,128)(2,1)} %param.7), channel_id=1, replica_groups=mesh['ia'=4,'ja'=4,'ka'=2] {'ja','ka'}, dimensions={1}, use_global_device_ids=true | all-gather | bytes 18432 | tf_op jit(solution)/shard_map/all_gather | solution.py:19
  21.8 0.7 copy-done.3
  22.4 21.9 %all_gather.9 = bf16[32,128]{0,1:T(8,128)(2,1)S(1)} all-gather(bf16[32,8]{0,1:T(8,128)(2,1)S(1)} %copy-done.3), channel_id=1, replica_groups=mesh['ia'=4,'ja'=4,'ka'=2] {'ia','ja'}, dimensions={1}, use_global_device_ids=true | all-gather | bytes 8704 | tf_op jit(solution)/shard_map/all_gather | solution.py:21
  44.4 0.7 copy-done.2
  45.1 30.6 %all_gather.11 = bf16[128,128]{0,1:T(8,128)(2,1)S(1)} all-gather(bf16[128,16]{0,1:T(8,128)(2,1)S(1)} %copy-done.2), channel_id=1, replica_groups=mesh['ia'=4,'ja'=4,'ka'=2] {'ia','ka'}, dimensions={1}, use_global_device_ids=true | all-gather | bytes 36864 | tf_op jit(solution)/shard_map/all_gather | solution.py:20
  75.7 1.4 multiply_convert_fusion.1
  77.2 0.9 copy-done.1
  78.4 1.0 fusion.16
  80.1 22.7 %psum.91 = f32[64,128]{1,0:T(8,128)S(1)} all-reduce(f32[64,128]{1,0:T(8,128)S(1)} %bitcast.75), channel_id=1, replica_groups=mesh['ia'=4,'ja'=4,'ka'=2] {'ja','ka'}, use_global_device_ids=true, to_apply=%region_0.0 | all-reduce | flops 8192 | bytes 65536 | tf_op jit(solution)/shard_map/psum | solution.py:45
  102.8 58.1 %psum.93 = f32[32,128]{1,0:T(8,128)S(1)} all-reduce(f32[32,128]{1,0:T(8,128)S(1)} %bitcast.78), channel_id=1, replica_groups=mesh['ia'=4,'ja'=4,'ka'=2] {'ia','ja'}, use_global_device_ids=true, to_apply=%region_4.0 | all-reduce | flops 4096 | bytes 32768 | tf_op jit(solution)/shard_map/psum | solution.py:47
  161.0 1.1 fusion.12
  162.5 1.0 fusion.17
  164.0 23.9 %psum.95 = f32[64,128]{1,0:T(8,128)S(1)} all-reduce(f32[64,128]{1,0:T(8,128)S(1)} %bitcast.76), channel_id=1, replica_groups=mesh['ia'=4,'ja'=4,'ka'=2] {'ja','ka'}, use_global_device_ids=true, to_apply=%region_7.0 | all-reduce | flops 8192 | bytes 65536 | tf_op jit(solution)/shard_map/psum | solution.py:45
  187.8 0.6 multiply_reduce_fusion.10
  188.4 57.7 %psum.97 = f32[32,128]{1,0:T(8,128)S(1)} all-reduce(f32[32,128]{1,0:T(8,128)S(1)} %bitcast.77), channel_id=1, replica_groups=mesh['ia'=4,'ja'=4,'ka'=2] {'ia','ja'}, use_global_device_ids=true, to_apply=%region_11.0 | all-reduce | flops 4096 | bytes 32768 | tf_op jit(solution)/shard_map/psum | solution.py:47
  246.2 0.7 multiply_reduce_fusion.13
  248.1 1.5 multiply_reduce_fusion.7
  252.3 36.9 %all-reduce = (f32[]{:T(128)}, f32[]{:T(128)}) all-reduce(f32[]{:T(128)S(6)} %add.125, f32[]{:T(128)S(6)} %add.132), channel_id=1, replica_groups=mesh['ia'=4,'ja'=4,'ka'=2] {'ia','ja','ka'}, use_global_device_ids=true, to_apply=%region_6.0 | all-reduce | flops 2 | bytes 16 | tf_op jit(solution)/shard_map/psum | solution.py:63
  290.5 0.6 multiply_reduce_fusion.12
  291.8 0.6 multiply_reduce_fusion.9
  292.4 0.6 multiply_reduce_fusion.6
  294.3 41.9 %psum.99 = f32[]{:T(128)} all-reduce(f32[]{:T(128)S(6)} %add.134), channel_id=1, replica_groups=mesh['ia'=4,'ja'=4,'ka'=2] {'ia','ja','ka'}, use_global_device_ids=true, to_apply=%region_17.0 | all-reduce | flops 1 | bytes 8 | tf_op jit(solution)/shard_map/psum | solution.py:63
  338.7 1.0 fusion.18
  339.6 59.3 %psum.102 = f32[32,128]{1,0:T(8,128)S(1)} all-reduce(f32[32,128]{1,0:T(8,128)S(1)} %bitcast.79), channel_id=1, replica_groups=mesh['ia'=4,'ja'=4,'ka'=2] {'ia','ja'}, use_global_device_ids=true, to_apply=%region_22.0 | all-reduce | flops 4096 | bytes 32768 | tf_op jit(solution)/shard_map/psum | solution.py:47
  400.3 23.2 %psum.100 = f32[64,128]{1,0:T(8,128)S(1)} all-reduce(f32[64,128]{1,0:T(8,128)S(1)} %bitcast.74), channel_id=1, replica_groups=mesh['ia'=4,'ja'=4,'ka'=2] {'ja','ka'}, use_global_device_ids=true, to_apply=%region_18.0 | all-reduce | flops 8192 | bytes 65536 | tf_op jit(solution)/shard_map/psum | solution.py:45
  423.5 0.6 fusion.8
  424.1 42.1 %all-reduce.9.cloned.1.call-done = f32[128,128]{1,0:T(8,128)} async-done(((f32[128,128]{1,0:T(8,128)}), f32[128,128]{1,0:T(8,128)}) %all-reduce.9.cloned.1.call-update) | async-done | bytes 65552 | tf_op jit(solution)/shard_map/psum | solution.py:46
  466.2 1.5 fusion.6
  469.0 40.3 %psum.103 = f32[]{:T(128)} all-reduce(f32[]{:T(128)S(6)} %add.144), channel_id=1, replica_groups=mesh['ia'=4,'ja'=4,'ka'=2] {'ia','ja','ka'}, use_global_device_ids=true, to_apply=%region_24.0 | all-reduce | flops 1 | bytes 8 | tf_op jit(solution)/shard_map/psum | solution.py:63
  510.7 0.7 copy.24
  511.5 0.7 copy.23
  512.2 0.7 copy.22
  (43 shorter events, 4.4 us)
Async XLA Ops:
  7.2 153.9 %all-reduce.5.cloned.1.call-start = ((), (), s32[]{:S(2)}) async-start(), calls=%async_computation | async-start | bytes 131072 | tf_op jit(solution)/shard_map/psum | solution.py:46
  21.8 0.7 copy-start.3
  44.4 0.7 copy-start.2
  77.0 1.0 copy-start.1
  79.4 168.7 %all-reduce.7.cloned.1.call-start = ((), (), s32[]{:S(2)}) async-start(), calls=%async_computation.1 | async-start | bytes 131072 | tf_op jit(solution)/shard_map/psum | solution.py:46
  163.8 302.5 %all-reduce.9.cloned.1.call-start = ((), (), s32[]{:S(2)}) async-start(), calls=%async_computation.2 | async-start | bytes 131072 | tf_op jit(solution)/shard_map/psum | solution.py:46
  188.4 59.7 %copy-start = (f32[128,128]{1,0:T(8,128)S(1)}, f32[128,128]{1,0:T(8,128)}, u32[]{:S(2)}) copy-start(f32[128,128]{1,0:T(8,128)} %all-reduce.5.cloned.1.call-done) | copy-start | bytes 196612
Sparse Core Ops, SparseCore 0:
  79.5 66.1 all-reduce.4
  163.9 66.5 all-reduce.6
  400.3 65.8 all-reduce.8
where the time goes:
time: 520 us; the launch traced here: 519 us
  blocking collectives  431 us (83%)
  waiting for transfers between devices  42.2 us (8%)
  between operations  25.8 us (5%)
  other arithmetic  9.88 us (2%)
  matrix products  6.15 us (1%)
    psum x3, blocking collectives, settle(): total_c = lax.psum(parts[2], ('ia', 'ja'))  175 us
    psum x3, blocking collectives, inner_sum(): return lax.psum(local_sum, ('ia', 'ja', 'ka'))  119 us
    psum x3, blocking collectives, settle(): total_a = lax.psum(parts[0], ('ja', 'ka'))  69.7 us
    psum x3, waiting for transfers between devices, settle(): total_b = lax.psum(parts[1], ('ia', 'ka'))  42.1 us
    all_gather x1, blocking collectives, local(): full_b = lax.all_gather(factor_b, ('ia', 'ka'), axis=1, tiled=True)  30.6 us
    all_gather x1, blocking collectives, local(): full_c = lax.all_gather(factor_c, ('ia', 'ja'), axis=1, tiled=True)  21.9 us
    all_gather x1, blocking collectives, local(): full_a = lax.all_gather(factor_a, ('ja', 'ka'), axis=1, tiled=True)  14.5 us
  transfers between devices with their start and end apart: 3, of which 1 were waited for; matrix products, arithmetic and copies ran while one was open for 1% of the time, Pallas kernels for 0%

commit v1 on v0

--- a/solution.py
+++ b/solution.py
@@ -43,7 +43,9 @@
 
     def settle(parts):
         total_a = lax.psum(parts[0], ("ja", "ka"))
-        total_b = lax.psum(parts[1], ("ia", "ka"))
+        total_b = parts[1]
+        for src_i in ("ka", "ia"):
+            total_b = lax.psum(total_b, src_i)
         total_c = lax.psum(parts[2], ("ia", "ja"))
         return (total_a, total_b, total_c)
 

time: 520 us -> 573 us (1.10)
  waiting for transfers between devices: 42.2 us -> 91.5 us
    psum x3 -> x6, waiting for transfers between devices: 42.1 us -> 91.4 us  [settle(): total_b = lax.psum(total_b, src_i)]
  transfers between devices with their start and end apart: 3 -> 6, of which waited for: 1 -> 3; matrix products, arithmetic and copies ran while one was open for 1% -> 1% of each run, Pallas kernels for 0% -> 0%
where the time goes in v1:
time: 573 us; the launch traced here: 572 us
  blocking collectives  434 us (76%)
  waiting for transfers between devices  91.5 us (16%)
  between operations  26.2 us (5%)
  other arithmetic  9.88 us (2%)
  matrix products  6.15 us (1%)
    psum x3, blocking collectives, settle(): total_c = lax.psum(parts[2], ('ia', 'ja'))  178 us
    psum x3, blocking collectives, inner_sum(): return lax.psum(local_sum, ('ia', 'ja', 'ka'))  119 us
    psum x6, waiting for transfers between devices, settle(): total_b = lax.psum(total_b, src_i)  91.4 us
    psum x3, blocking collectives, settle(): total_a = lax.psum(parts[0], ('ja', 'ka'))  69.2 us
    all_gather x1, blocking collectives, local(): full_b = lax.all_gather(factor_b, ('ia', 'ka'), axis=1, tiled=True)  30.6 us
    all_gather x1, blocking collectives, local(): full_c = lax.all_gather(factor_c, ('ia', 'ja'), axis=1, tiled=True)  21.9 us
    all_gather x1, blocking collectives, local(): full_a = lax.all_gather(factor_a, ('ja', 'ka'), axis=1, tiled=True)  14.5 us
  transfers between devices with their start and end apart: 6, of which 3 were waited for; matrix products, arithmetic and copies ran while one was open for 1% of the time, Pallas kernels for 0%

profile of v1, /device:TPU:0, one launch (start us, length us, event | category | flops | bytes accessed | tf_op | source)
XLA Modules:
  0.0 572.4 jit_solution(304773239386209187)
XLA Ops:
  7.2 14.5 %all_gather.10 = bf16[64,128]{0,1:T(8,128)(2,1)S(1)} all-gather(bf16[64,16]{0,1:T(8,128)(2,1)} %param.7), channel_id=1, replica_groups=mesh['ia'=4,'ja'=4,'ka'=2] {'ja','ka'}, dimensions={1}, use_global_device_ids=true | all-gather | bytes 18432 | tf_op jit(solution)/shard_map/all_gather | solution.py:19
  21.8 0.7 copy-done.3
  22.4 21.9 %all_gather.9 = bf16[32,128]{0,1:T(8,128)(2,1)S(1)} all-gather(bf16[32,8]{0,1:T(8,128)(2,1)S(1)} %copy-done.3), channel_id=1, replica_groups=mesh['ia'=4,'ja'=4,'ka'=2] {'ia','ja'}, dimensions={1}, use_global_device_ids=true | all-gather | bytes 8704 | tf_op jit(solution)/shard_map/all_gather | solution.py:21
  44.4 0.7 copy-done.2
  45.1 30.6 %all_gather.11 = bf16[128,128]{0,1:T(8,128)(2,1)S(1)} all-gather(bf16[128,16]{0,1:T(8,128)(2,1)S(1)} %copy-done.2), channel_id=1, replica_groups=mesh['ia'=4,'ja'=4,'ka'=2] {'ia','ka'}, dimensions={1}, use_global_device_ids=true | all-gather | bytes 36864 | tf_op jit(solution)/shard_map/all_gather | solution.py:20
  75.7 1.4 multiply_convert_fusion.1
  77.2 0.9 copy-done.1
  78.4 1.0 fusion.16
  80.1 22.5 %psum.112 = f32[64,128]{1,0:T(8,128)S(1)} all-reduce(f32[64,128]{1,0:T(8,128)S(1)} %bitcast.75), channel_id=1, replica_groups=mesh['ia'=4,'ja'=4,'ka'=2] {'ja','ka'}, use_global_device_ids=true, to_apply=%region_0.0 | all-reduce | flops 8192 | bytes 65536 | tf_op jit(solution)/shard_map/psum | solution.py:45
  102.6 58.1 %psum.115 = f32[32,128]{1,0:T(8,128)S(1)} all-reduce(f32[32,128]{1,0:T(8,128)S(1)} %bitcast.78), channel_id=1, replica_groups=mesh['ia'=4,'ja'=4,'ka'=2] {'ia','ja'}, use_global_device_ids=true, to_apply=%region_5.0 | all-reduce | flops 4096 | bytes 32768 | tf_op jit(solution)/shard_map/psum | solution.py:49
  161.0 31.6 %all-reduce.10.cloned.1.call-done = f32[128,128]{1,0:T(8,128)} async-done(((f32[128,128]{1,0:T(8,128)}), f32[128,128]{1,0:T(8,128)}) %all-reduce.10.cloned.1.call-update) | async-done | bytes 65552 | tf_op jit(solution)/shard_map/psum | solution.py:48
  192.6 1.1 fusion.12
  194.0 1.0 fusion.17
  195.5 23.9 %psum.117 = f32[64,128]{1,0:T(8,128)S(1)} all-reduce(f32[64,128]{1,0:T(8,128)S(1)} %bitcast.76), channel_id=1, replica_groups=mesh['ia'=4,'ja'=4,'ka'=2] {'ja','ka'}, use_global_device_ids=true, to_apply=%region_8.0 | all-reduce | flops 8192 | bytes 65536 | tf_op jit(solution)/shard_map/psum | solution.py:45
  219.4 0.6 multiply_reduce_fusion.10
  220.0 60.1 %psum.120 = f32[32,128]{1,0:T(8,128)S(1)} all-reduce(f32[32,128]{1,0:T(8,128)S(1)} %bitcast.77), channel_id=1, replica_groups=mesh['ia'=4,'ja'=4,'ka'=2] {'ia','ja'}, use_global_device_ids=true, to_apply=%region_13.0 | all-reduce | flops 4096 | bytes 32768 | tf_op jit(solution)/shard_map/psum | solution.py:49
  280.2 0.7 multiply_reduce_fusion.13
  282.1 28.3 %all-reduce.14.cloned.1.call-done = f32[128,128]{1,0:T(8,128)} async-done(((f32[128,128]{1,0:T(8,128)}), f32[128,128]{1,0:T(8,128)}) %all-reduce.14.cloned.1.call-update) | async-done | bytes 65552 | tf_op jit(solution)/shard_map/psum | solution.py:48
  310.5 1.5 multiply_reduce_fusion.7
  314.7 40.1 %all-reduce = (f32[]{:T(128)}, f32[]{:T(128)}) all-reduce(f32[]{:T(128)S(6)} %add.131, f32[]{:T(128)S(6)} %add.138), channel_id=1, replica_groups=mesh['ia'=4,'ja'=4,'ka'=2] {'ia','ja','ka'}, use_global_device_ids=true, to_apply=%region_7.0 | all-reduce | flops 2 | bytes 16 | tf_op jit(solution)/shard_map/psum | solution.py:65
  357.3 0.6 multiply_reduce_fusion.9
  357.9 0.6 multiply_reduce_fusion.6
  359.9 39.2 %psum.122 = f32[]{:T(128)} all-reduce(f32[]{:T(128)S(6)} %add.140), channel_id=1, replica_groups=mesh['ia'=4,'ja'=4,'ka'=2] {'ia','ja','ka'}, use_global_device_ids=true, to_apply=%region_19.0 | all-reduce | flops 1 | bytes 8 | tf_op jit(solution)/shard_map/psum | solution.py:65
  401.5 1.0 fusion.18
  402.5 60.2 %psum.126 = f32[32,128]{1,0:T(8,128)S(1)} all-reduce(f32[32,128]{1,0:T(8,128)S(1)} %bitcast.79), channel_id=1, replica_groups=mesh['ia'=4,'ja'=4,'ka'=2] {'ia','ja'}, use_global_device_ids=true, to_apply=%region_25.0 | all-reduce | flops 4096 | bytes 32768 | tf_op jit(solution)/shard_map/psum | solution.py:49
  464.1 22.9 %psum.123 = f32[64,128]{1,0:T(8,128)S(1)} all-reduce(f32[64,128]{1,0:T(8,128)S(1)} %bitcast.74), channel_id=1, replica_groups=mesh['ia'=4,'ja'=4,'ka'=2] {'ja','ka'}, use_global_device_ids=true, to_apply=%region_20.0 | all-reduce | flops 8192 | bytes 65536 | tf_op jit(solution)/shard_map/psum | solution.py:45
  487.6 31.4 %all-reduce.18.cloned.1.call-done = f32[128,128]{1,0:T(8,128)} async-done(((f32[128,128]{1,0:T(8,128)}), f32[128,128]{1,0:T(8,128)}) %all-reduce.18.cloned.1.call-update) | async-done | bytes 65552 | tf_op jit(solution)/shard_map/psum | solution.py:48
  519.1 1.5 fusion.6
  521.8 40.1 %psum.127 = f32[]{:T(128)} all-reduce(f32[]{:T(128)S(6)} %add.150), channel_id=1, replica_groups=mesh['ia'=4,'ja'=4,'ka'=2] {'ia','ja','ka'}, use_global_device_ids=true, to_apply=%region_27.0 | all-reduce | flops 1 | bytes 8 | tf_op jit(solution)/shard_map/psum | solution.py:65
  563.3 0.7 copy.24
  564.1 0.7 copy.23
  564.9 0.7 copy.22
  (52 shorter events, 5.8 us)
Async XLA Ops:
  7.2 153.6 %all-reduce.8.cloned.1.call-start = ((), (), s32[]{:S(2)}) async-start(), calls=%async_computation | async-start | bytes 131072 | tf_op jit(solution)/shard_map/psum | solution.py:48
  21.8 0.7 copy-start.3
  44.4 0.7 copy-start.2
  77.0 1.0 copy-start.1
  79.4 113.2 %all-reduce.10.cloned.1.call-start = ((), (), s32[]{:S(2)}) async-start(), calls=%async_computation.1 | async-start | bytes 131072 | tf_op jit(solution)/shard_map/psum | solution.py:48
  160.8 119.4 %all-reduce.12.cloned.1.call-start = ((), (), s32[]{:S(2)}) async-start(), calls=%async_computation.2 | async-start | bytes 131072 | tf_op jit(solution)/shard_map/psum | solution.py:48
  195.3 115.2 %all-reduce.14.cloned.1.call-start = ((), (), s32[]{:S(2)}) async-start(), calls=%async_computation.3 | async-start | bytes 131072 | tf_op jit(solution)/shard_map/psum | solution.py:48
  280.1 30.4 %copy-start = (f32[128,128]{1,0:T(8,128)S(1)}, f32[128,128]{1,0:T(8,128)}, u32[]{:S(2)}) copy-start(f32[128,128]{1,0:T(8,128)} %all-reduce.10.cloned.1.call-done) | copy-start | bytes 196612
  280.1 206.9 %all-reduce.16.cloned.1.call-start = ((), (), s32[]{:S(2)}) async-start(), calls=%async_computation.4 | async-start | bytes 131072 | tf_op jit(solution)/shard_map/psum | solution.py:48
  462.7 56.4 %all-reduce.18.cloned.1.call-start = ((), (), s32[]{:S(2)}) async-start(), calls=%async_computation.5 | async-start | bytes 131072 | tf_op jit(solution)/shard_map/psum | solution.py:48
Sparse Core Ops, SparseCore 0:
  79.5 17.8 all-reduce.7
  160.9 31.6 all-reduce.9
  195.4 20.5 all-reduce.11
  280.3 30.1 all-reduce.13
  462.8 17.2 all-reduce.15
  487.1 31.8 all-reduce.17
